TPU v7x, 32 devices: a whole 2x2x4 slice. The times are simulated.
32 devices in a mesh: shard: 4 (over z), ctx: 4 (over x, core), tp: 2 (over y).
Axes of the slice: x: 2, y: 2, z: 4, core: 2. Of those that a mesh axis runs over, the one named last changes fastest.
Arguments:
- layer_in: bfloat16 [3072, 2048], P(('shard', 'ctx')), may hold values from -6 to 6
- w_qkv: bfloat16 [6144, 2048], P(('shard', 'ctx'), 'tp'), may hold values from -0.125 to 0.125
- w_out: bfloat16 [2048, 2048], P(('shard', 'ctx'), 'tp'), may hold values from -1.5 to 1.5
- norm_gains: bfloat16 [2048, 4], P(('shard', 'ctx')), may hold values from 0.25 to 1.75
- router: bfloat16 [2048, 16], P(('shard', 'ctx')), may hold values from -0.0625 to 0.0625
- w_gate_up: bfloat16 [16, 2048, 2, 1024], P(('shard', 'ctx'), None, None, 'tp'), may hold values from -0.125 to 0.125
- w_down: bfloat16 [16, 2048, 1024], P(('shard', 'ctx'), None, 'tp'), may hold values from -0.75 to 0.75
- routes: int32 [3072, 8], P(('shard', 'ctx')), may hold values from 0 to 15, all different within a row; in each aligned block of 192 rows (0 to 191, 192 to 383, ...) at most 120 rows name the same one
- lengths: int32 [4, 3], P('shard'), may hold values from 1 to 614, 768 in all within a row
- token_order: int32 [4, 768], P('shard'), may hold values from 0 to 767, each once within a row
- out_grad: bfloat16 [3072, 2048], P(('shard', 'ctx')), may hold values from -6 to 6
Outputs:
- output: bfloat16 [3072, 2048], P(('shard', 'ctx'))
- input_grad: float32 [3072, 2048], P(('shard', 'ctx'))
- qkv_grad: float32 [6144, 2048], P(('shard', 'ctx'), 'tp')
- out_proj_grad: float32 [2048, 2048], P(('shard', 'ctx'), 'tp')
- gains_grad: float32 [2048, 4], P(('shard', 'ctx'))
- router_grad: float32 [2048, 16], P(('shard', 'ctx'))
- gate_up_grad: float32 [16, 2048, 2, 1024], P(('shard', 'ctx'), None, None, 'tp')
- down_grad: float32 [16, 2048, 1024], P(('shard', 'ctx'), None, 'tp')
Inputs may be any that keep to these rules, and one draw needn't show every extreme that they name: `routes`: each row names 8 different experts. Among the 192 rows of one device no expert is named more than 120 times, a bound that some block reaches there. Each row holds the lengths of the 3 sequences of one group; they sum to 768 and the longest is exactly 614. `token_order`: each row is a permutation of the places of its group.
All inputs are finite; a program needn't handle non-finite values.
Results may differ from a plain program's by a relative error of at most 0.017.
Values may be sent and summed in bfloat16 or wider, within the bound.
No kernel may reach another device: no remote copies, remote signals or barrier semaphores. Data moves between devices by JAX's collectives and lax.ppermute only.
A program may use at most 320 MiB of HBM per device.

v0:
```python
import jax
import jax.numpy as jnp
from jax import lax
from jax.sharding import PartitionSpec as P

HEAD = 128
norm_eps = 1e-05
rope_base = 10000.0
masked_score = -1e30


def places_info(order_row, length_row):
    seq_ends = jnp.cumsum(length_row)
    seq_starts = seq_ends - length_row
    sequence = jnp.sum((order_row[:, None] >= seq_ends[None, :]).astype(jnp.int32), axis=1)
    picker = jnp.arange(length_row.shape[0], dtype=jnp.int32)[None, :] == sequence[:, None]
    first_place = jnp.sum(jnp.where(picker, seq_starts[None, :], 0), axis=1)
    return (sequence, order_row - first_place)


def rope_tables(place_pos, head_size):
    freq_index = jnp.arange(head_size // 2, dtype=jnp.float32)
    inverse = 1.0 / rope_base ** (freq_index * 2.0 / head_size)
    angle = place_pos.astype(jnp.float32)[:, None] * inverse[None, :]
    cosine = jnp.cos(angle)
    sine = jnp.sin(angle)
    return (jnp.concatenate([cosine, cosine], 1), jnp.concatenate([sine, sine], 1))


def rotate(values_in, cosine, sine):
    half_width = values_in.shape[-1] // 2
    turned = jnp.concatenate([-values_in[..., half_width:], values_in[..., :half_width]], -1)
    return values_in * cosine[:, None, :] + turned * sine[:, None, :]


def rotate_back(grad_in, cosine, sine):
    half_width = grad_in.shape[-1] // 2
    scaled = grad_in * sine[:, None, :]
    return grad_in * cosine[:, None, :] + jnp.concatenate(
        [scaled[..., half_width:], -scaled[..., :half_width]], -1
    )


def slot_index(expert_flat, expert_count, capacity):
    chosen = (expert_flat[:, None] == jnp.arange(expert_count, dtype=jnp.int32)[None, :]).astype(
        jnp.int32
    )
    before = jnp.cumsum(chosen, axis=0) - chosen
    slot_num = jnp.sum(before * chosen, axis=1)
    return expert_flat * capacity + slot_num


def local(
    layer_in,
    w_qkv,
    w_out,
    norm_gains,
    router,
    w_gate_up,
    w_down,
    routes,
    lengths,
    token_order,
    out_grad,
):
    tokens, width = layer_in.shape
    topk = routes.shape[1]
    experts = router.shape[1]
    capacity = max(2, tokens * topk * 5 // (4 * experts))
    qkv_all, out_all, gains_all, router_all = (
        lax.all_gather(w_qkv, ("shard", "ctx"), axis=0, tiled=True),
        lax.all_gather(w_out, ("shard", "ctx"), axis=0, tiled=True),
        lax.all_gather(norm_gains, ("shard", "ctx"), axis=0, tiled=True),
        lax.all_gather(router, ("shard", "ctx"), axis=0, tiled=True),
    )
    half_width = qkv_all.shape[1]
    full_heads = half_width * lax.axis_size("tp")
    head_count = half_width // HEAD
    tp_index = lax.axis_index("tp")
    ctx_index = lax.axis_index("ctx")
    gains_f = gains_all.astype(jnp.float32)
    gain_in = gains_f[:, 0]
    gain_mid = gains_f[:, 1]
    gain_q = lax.dynamic_slice_in_dim(gains_f[:, 2], tp_index * half_width, half_width)
    gain_k = lax.dynamic_slice_in_dim(gains_f[:, 3], tp_index * half_width, half_width)
    score_scale = HEAD ** (-0.5)
    group_len = token_order.shape[1]
    seq_all, pos_all = places_info(token_order[0], lengths[0])
    seq_mine = lax.dynamic_slice_in_dim(seq_all, ctx_index * tokens, tokens)
    pos_mine = lax.dynamic_slice_in_dim(pos_all, ctx_index * tokens, tokens)
    cosine, sine = rope_tables(pos_mine, HEAD)
    visible = (seq_mine[:, None] == seq_all[None, :]) & (pos_all[None, :] <= pos_mine[:, None])
    layer_f = layer_in.astype(jnp.float32)
    rate_in = lax.rsqrt(jnp.mean(layer_f * layer_f, axis=-1, keepdims=True) + norm_eps)
    in_hat = layer_f * rate_in
    in_norm = in_hat * gain_in
    in_low = in_norm.astype(jnp.bfloat16)
    qkv_mats = qkv_all.reshape(3, width, half_width)
    projected = jnp.einsum("td,jdh->tjh", in_low, qkv_mats, preferred_element_type=jnp.float32)
    q_raw = projected[:, 0]
    k_raw = projected[:, 1]
    v_raw = projected[:, 2]
    square_q, square_k = lax.psum(
        (jnp.sum(q_raw * q_raw, axis=1), jnp.sum(k_raw * k_raw, axis=1)), "tp"
    )
    rate_q = lax.rsqrt(square_q / full_heads + norm_eps)[:, None]
    rate_k = lax.rsqrt(square_k / full_heads + norm_eps)[:, None]
    q_hat = q_raw * rate_q
    k_hat = k_raw * rate_k
    q_low = rotate((q_hat * gain_q).reshape(tokens, head_count, HEAD), cosine, sine).astype(
        jnp.bfloat16
    )
    k_low = (
        rotate((k_hat * gain_k).reshape(tokens, head_count, HEAD), cosine, sine)
        .astype(jnp.bfloat16)
        .reshape(tokens, half_width)
    )
    v_low = v_raw.astype(jnp.bfloat16)
    key_rows, value_rows = (
        lax.all_gather(k_low, "ctx", axis=0, tiled=True),
        lax.all_gather(v_low, "ctx", axis=0, tiled=True),
    )
    key_heads = key_rows.reshape(group_len, head_count, HEAD)
    value_heads = value_rows.reshape(group_len, head_count, HEAD)
    scores = (
        jnp.einsum("qhd,khd->hqk", q_low, key_heads, preferred_element_type=jnp.float32)
        * score_scale
    )
    scores = jnp.where(visible[None], scores, masked_score)
    row_max = jnp.max(scores, axis=-1, keepdims=True)
    shifted = jnp.exp(scores - row_max)
    row_sum = jnp.sum(shifted, axis=-1, keepdims=True)
    weights = shifted / row_sum
    log_total = row_max + jnp.log(row_sum)
    mixed = jnp.einsum(
        "hqk,khd->qhd",
        weights.astype(jnp.bfloat16),
        value_heads,
        preferred_element_type=jnp.float32,
    )
    mixed_low = mixed.reshape(tokens, half_width).astype(jnp.bfloat16)
    attn_part = lax.dot_general(
        mixed_low, out_all, (((1,), (1,)), ((), ())), preferred_element_type=jnp.float32
    )
    attn = lax.psum(attn_part, "tp")
    resid = layer_f + attn
    rate_mid = lax.rsqrt(jnp.mean(resid * resid, axis=-1, keepdims=True) + norm_eps)
    mid_hat = resid * rate_mid
    mid_norm = mid_hat * gain_mid
    mid_low = mid_norm.astype(jnp.bfloat16)
    router_f = router_all.astype(jnp.float32)
    logits = jnp.dot(mid_norm, router_f, precision=lax.Precision.HIGHEST)
    chosen = routes[:, :, None] == jnp.arange(experts, dtype=jnp.int32)[None, None, :]
    picked = jnp.sum(jnp.where(chosen, logits[:, None, :], 0.0), axis=-1)
    picked_max = jnp.max(picked, axis=-1, keepdims=True)
    picked_exp = jnp.exp(picked - picked_max)
    gates = picked_exp / jnp.sum(picked_exp, axis=-1, keepdims=True)
    slot_dest = slot_index(routes.reshape(-1), experts, capacity)
    token_of = jnp.arange(tokens * topk, dtype=jnp.int32) // topk
    slot_token = jnp.full((experts * capacity,), -1, jnp.int32).at[slot_dest].set(token_of)
    filled = slot_token >= 0
    safe_token = jnp.maximum(slot_token, 0)
    gate_slot = jnp.zeros((experts * capacity,), jnp.float32).at[slot_dest].set(gates.reshape(-1))
    send_mid = jnp.where(filled[:, None], mid_low[safe_token], jnp.zeros((), jnp.bfloat16)).reshape(
        experts, capacity, width
    )
    send_grad = (
        (gate_slot[:, None] * out_grad[safe_token].astype(jnp.float32))
        .astype(jnp.bfloat16)
        .reshape(experts, capacity, width)
    )
    recv_mid, recv_grad = (
        lax.all_to_all(send_mid, ("shard", "ctx"), split_axis=0, concat_axis=1, tiled=True),
        lax.all_to_all(send_grad, ("shard", "ctx"), split_axis=0, concat_axis=1, tiled=True),
    )
    gate_up = jnp.einsum("erd,edjf->erjf", recv_mid, w_gate_up, preferred_element_type=jnp.float32)
    gate_val = gate_up[:, :, 0]
    up_val = gate_up[:, :, 1]
    gate_sig = jax.nn.sigmoid(gate_val)
    gate_act = gate_val * gate_sig
    hidden_act = (gate_act * up_val).astype(jnp.bfloat16)
    expert_part = jnp.einsum("erf,edf->erd", hidden_act, w_down, preferred_element_type=jnp.float32)
    hidden_grad = jnp.einsum("erd,edf->erf", recv_grad, w_down, preferred_element_type=jnp.float32)
    gate_grad = hidden_grad * up_val * gate_sig * (1.0 + gate_val * (1.0 - gate_sig))
    up_grad = hidden_grad * gate_act
    both_grad = jnp.stack([gate_grad, up_grad], axis=2).astype(jnp.bfloat16)
    mid_part = jnp.einsum(
        "erjf,edjf->erd", both_grad, w_gate_up, preferred_element_type=jnp.float32
    )
    gate_up_grad = jnp.einsum(
        "erd,erjf->edjf", recv_mid, both_grad, preferred_element_type=jnp.float32
    )
    down_grad = jnp.einsum(
        "erd,erf->edf", recv_grad, hidden_act, preferred_element_type=jnp.float32
    )
    out_grad_f = out_grad.astype(jnp.float32)
    back_rows, back_grads = (
        lax.all_to_all(expert_part, ("shard", "ctx"), split_axis=1, concat_axis=0, tiled=True),
        lax.all_to_all(mid_part, ("shard", "ctx"), split_axis=1, concat_axis=0, tiled=True),
    )
    columns = back_rows.shape[-1]
    rows_y = back_rows.reshape(experts * capacity, columns)[slot_dest].reshape(
        tokens, topk, columns
    )
    rows_g = back_grads.reshape(experts * capacity, columns)[slot_dest].reshape(
        tokens, topk, columns
    )
    mixture_part = jnp.sum(gates[:, :, None] * rows_y, axis=1)
    grad_part = jnp.sum(rows_g, axis=1)
    score_part = jnp.sum(out_grad_f[:, None, :] * rows_y, axis=2)
    mixture_part, grad_part, score_part = (mixture_part, grad_part, score_part)
    mixture, mid_grad, score_total = lax.psum((mixture_part, grad_part, score_part), "tp")
    output = (resid + mixture).astype(jnp.bfloat16)
    picked_grad = gates * (score_total - jnp.sum(gates * score_total, axis=1, keepdims=True))
    logit_grad = jnp.sum(jnp.where(chosen, picked_grad[:, :, None], 0.0), axis=1)
    router_grad = lax.dot_general(
        mid_norm, logit_grad, (((0,), (0,)), ((), ())), precision=lax.Precision.HIGHEST
    )
    mid_grad = mid_grad + lax.dot_general(
        logit_grad, router_f, (((1,), (1,)), ((), ())), precision=lax.Precision.HIGHEST
    )
    mid_scaled = gain_mid * mid_grad
    resid_grad = out_grad_f + rate_mid * (
        mid_scaled - mid_hat * jnp.mean(mid_hat * mid_scaled, axis=-1, keepdims=True)
    )
    gain_mid_grad = jnp.sum(mid_grad * mid_hat, axis=0)
    attn_low = resid_grad.astype(jnp.bfloat16)
    out_proj_grad = lax.dot_general(
        attn_low, mixed_low, (((0,), (0,)), ((), ())), preferred_element_type=jnp.float32
    )
    mixed_grad = (
        jnp.dot(attn_low, out_all, preferred_element_type=jnp.float32)
        .astype(jnp.bfloat16)
        .reshape(tokens, head_count, HEAD)
    )
    again = (
        jnp.einsum("qhd,khd->hqk", q_low, key_heads, preferred_element_type=jnp.float32)
        * score_scale
    )
    again = jnp.where(visible[None], again, masked_score)
    weights_again = jnp.exp(again - log_total)
    weights_low = weights_again.astype(jnp.bfloat16)
    weight_grad = jnp.einsum(
        "qhd,khd->hqk", mixed_grad, value_heads, preferred_element_type=jnp.float32
    )
    score_grad = weights_again * (
        weight_grad - jnp.sum(weights_again * weight_grad, axis=-1, keepdims=True)
    )
    score_low = score_grad.astype(jnp.bfloat16)
    q_grad = (
        jnp.einsum("hqk,khd->qhd", score_low, key_heads, preferred_element_type=jnp.float32)
        * score_scale
    )
    k_part = (
        jnp.einsum("hqk,qhd->khd", score_low, q_low, preferred_element_type=jnp.float32)
        * score_scale
    )
    v_part = jnp.einsum("hqk,qhd->khd", weights_low, mixed_grad, preferred_element_type=jnp.float32)
    k_grad, v_grad = (
        lax.psum_scatter(
            k_part.reshape(group_len, half_width), "ctx", scatter_dimension=0, tiled=True
        ),
        lax.psum_scatter(
            v_part.reshape(group_len, half_width), "ctx", scatter_dimension=0, tiled=True
        ),
    )
    q_in = rotate_back(q_grad, cosine, sine).reshape(tokens, half_width)
    k_in = rotate_back(k_grad.reshape(tokens, head_count, HEAD), cosine, sine).reshape(
        tokens, half_width
    )
    q_scaled = gain_q * q_in
    k_scaled = gain_k * k_in
    inner_q, inner_k = lax.psum(
        (jnp.sum(q_scaled * q_hat, axis=1), jnp.sum(k_scaled * k_hat, axis=1)), "tp"
    )
    q_raw_grad = rate_q * (q_scaled - q_hat * (inner_q / full_heads)[:, None])
    k_raw_grad = rate_k * (k_scaled - k_hat * (inner_k / full_heads)[:, None])
    gain_pair = jnp.stack([jnp.sum(q_in * q_hat, axis=0), jnp.sum(k_in * k_hat, axis=0)], axis=1)
    qk_gain_part = lax.dynamic_update_slice(
        jnp.zeros((width, 2), jnp.float32), gain_pair, (tp_index * half_width, 0)
    )
    raw_grad = jnp.stack([q_raw_grad, k_raw_grad, v_grad], axis=1).astype(jnp.bfloat16)
    qkv_grad = jnp.einsum(
        "td,tjh->jdh", in_low, raw_grad, preferred_element_type=jnp.float32
    ).reshape(3 * width, half_width)
    norm_part = jnp.einsum("tjh,jdh->td", raw_grad, qkv_mats, preferred_element_type=jnp.float32)
    in_norm_grad, qk_gain_grad = (
        lax.psum(norm_part.astype(jnp.bfloat16), "tp").astype(jnp.float32),
        lax.psum(qk_gain_part.astype(jnp.bfloat16), "tp").astype(jnp.float32),
    )
    in_scaled = gain_in * in_norm_grad
    input_grad = resid_grad + rate_in * (
        in_scaled - in_hat * jnp.mean(in_hat * in_scaled, axis=-1, keepdims=True)
    )
    gain_in_grad = jnp.sum(in_norm_grad * in_hat, axis=0)
    gains_grad = jnp.stack(
        [gain_in_grad, gain_mid_grad, qk_gain_grad[:, 0], qk_gain_grad[:, 1]], axis=1
    )
    qkv_owned, out_owned, gains_owned, router_owned = (
        lax.psum_scatter(qkv_grad, ("shard", "ctx"), scatter_dimension=0, tiled=True),
        lax.psum_scatter(out_proj_grad, ("shard", "ctx"), scatter_dimension=0, tiled=True),
        lax.psum_scatter(gains_grad, ("shard", "ctx"), scatter_dimension=0, tiled=True),
        lax.psum_scatter(router_grad, ("shard", "ctx"), scatter_dimension=0, tiled=True),
    )
    return (
        output,
        input_grad,
        qkv_owned,
        out_owned,
        gains_owned,
        router_owned,
        gate_up_grad,
        down_grad,
    )


def solution(mesh):
    in_specs = (
        P(("shard", "ctx"), None),
        P(("shard", "ctx"), "tp"),
        P(("shard", "ctx"), "tp"),
        P(("shard", "ctx"), None),
        P(("shard", "ctx"), None),
        P(("shard", "ctx"), None, None, "tp"),
        P(("shard", "ctx"), None, "tp"),
        P(("shard", "ctx"), None),
        P("shard", None),
        P("shard", None),
        P(("shard", "ctx"), None),
    )
    out_specs = (
        P(("shard", "ctx"), None),
        P(("shard", "ctx"), None),
        P(("shard", "ctx"), "tp"),
        P(("shard", "ctx"), "tp"),
        P(("shard", "ctx"), None),
        P(("shard", "ctx"), None),
        P(("shard", "ctx"), None, None, "tp"),
        P(("shard", "ctx"), None, "tp"),
    )
    return jax.shard_map(local, mesh=mesh, in_specs=in_specs, out_specs=out_specs, check_vma=False)
```

profile of v0, /device:TPU:0, one launch (start us, length us, event | category | flops | bytes accessed | tf_op | source)
XLA Modules:
  0.0 2155.8 jit_solution(1457848799466026686)
XLA Ops:
  10.4 23.8 %all_gather.18 = bf16[2048,4]{0,1:T(4,128)(2,1)S(1)} all-gather(bf16[128,4]{0,1:T(4,128)(2,1)} %param.14), channel_id=1, replica_groups=mesh['shard'=4,'ctx'=4,'tp'=2] {'shard','ctx'}, dimensions={0}, use_global_device_ids=true | all-gather | bytes 17408 | tf_op jit(solution)/shard_map/all_gather | solution.py:73
  37.0 76.5 %all-gather.6.cloned.1.call-done = bf16[6144,1024]{1,0:T(8,128)(2,1)} async-done(((bf16[384,1024]{1,0:T(8,128)(2,1)}), bf16[6144,1024]{1,0:T(8,128)(2,1)}) %all-gather.6.cloned.1.call-update) | async-done | bytes 12582928 | tf_op jit(solution)/shard_map/all_gather | solution.py:71
  143.6 18.0 all-gather.8.cloned.1.call-done
  168.4 45.7 %all-gather.10.cloned.1.call-done = bf16[2048,1024]{1,0:T(8,128)(2,1)} async-done(((bf16[128,1024]{1,0:T(8,128)(2,1)}), bf16[2048,1024]{1,0:T(8,128)(2,1)}) %all-gather.10.cloned.1.call-update) | async-done | bytes 4194320 | tf_op jit(solution)/shard_map/all_gather | solution.py:72
  231.5 37.7 %all-reduce.7.cloned.1.call-done = f32[192,2048]{1,0:T(8,128)} async-done(((f32[192,2048]{1,0:T(8,128)}), f32[192,2048]{1,0:T(8,128)}) %all-reduce.7.cloned.1.call-update) | async-done | bytes 1572880 | tf_op jit(solution)/shard_map/psum | solution.py:145
  302.5 134.7 %all_gather.23 = bf16[2048,16]{0,1:T(8,128)(2,1)S(1)} all-gather(bf16[128,16]{0,1:T(8,128)(2,1)S(1)} %copy-done.70), channel_id=1, replica_groups=mesh['shard'=4,'ctx'=4,'tp'=2] {'shard','ctx'}, dimensions={0}, use_global_device_ids=true | all-gather | bytes 69632 | tf_op jit(solution)/shard_map/all_gather | solution.py:74
  455.7 42.1 %all-to-all-start.2 = ((bf16[16,120,2048]{2,1,0:T(8,128)(2,1)}), bf16[16,120,2048]{2,1,0:T(8,128)(2,1)}, u32[]{:S(2)}, u32[]{:S(2)}) async-start(bf16[16,120,2048]{2,1,0:T(8,128)(2,1)} %fusion), calls=%async_computation.2 | async-start | bytes 15728640 | tf_op jit(solution)/shard_map/all_to_all | solution.py:174
  497.8 13.8 convolution_bitcast_fusion.4
  511.6 127.7 %all-to-all-done.2 = bf16[16,120,2048]{2,1,0:T(8,128)(2,1)} async-done(((bf16[16,120,2048]{2,1,0:T(8,128)(2,1)}), bf16[16,120,2048]{2,1,0:T(8,128)(2,1)}, u32[]{:S(2)}, u32[]{:S(2)}) %all-to-all-start.2) | async-done | bytes 7864352 | tf_op jit(solution)/shard_map/all_to_all | solution.py:174
  639.3 12.0 fusion.31
  651.3 10.6 convolution_bitcast_fusion
  662.0 22.7 %copy.137 = f32[1,1920,2048]{2,0,1:T(1,128)} copy(f32[1,1920,2048]{2,1,0:T(8,128)S(1)} %convolution_bitcast_fusion) | data formatting | bytes 31457280 | tf_op jit(solution)/shard_map/erjf,edjf->erd/dot_general | solution.py:187
  684.6 35.3 %all-to-all-start.3 = ((f32[1,1920,2048]{2,0,1:T(1,128)}), f32[1,1920,2048]{2,0,1:T(1,128)}, u32[]{:S(2)}, u32[]{:S(2)}) async-start(f32[1,1920,2048]{2,0,1:T(1,128)} %copy.137), calls=%async_computation.3 | async-start | bytes 31457280 | tf_op jit(solution)/shard_map/all_to_all | solution.py:199
  728.8 22.6 %copy.134 = f32[1,1920,2048]{2,0,1:T(1,128)} copy(f32[1,1920,2048]{2,1,0:T(8,128)S(1)} %convolution_bitcast_fusion.1) | data formatting | bytes 31457280 | tf_op jit(solution)/shard_map/erf,edf->erd/dot_general | solution.py:182
  751.5 246.8 %all-to-all-done.3 = f32[1,1920,2048]{2,0,1:T(1,128)} async-done(((f32[1,1920,2048]{2,0,1:T(1,128)}), f32[1,1920,2048]{2,0,1:T(1,128)}, u32[]{:S(2)}, u32[]{:S(2)}) %all-to-all-start.3) | async-done | bytes 15728672 | tf_op jit(solution)/shard_map/all_to_all | solution.py:199
  998.3 66.0 %all-to-all-start.1 = ((f32[1,1920,2048]{2,0,1:T(1,128)}), f32[1,1920,2048]{2,0,1:T(1,128)}, u32[]{:S(2)}, u32[]{:S(2)}) async-start(f32[1,1920,2048]{2,0,1:T(1,128)} %copy.134), calls=%async_computation.1 | async-start | bytes 31457280 | tf_op jit(solution)/shard_map/all_to_all | solution.py:198
  1064.8 18.7 copy.240
  1083.5 18.4 gather_fusion.3
  1110.6 232.1 %all-to-all-done.1 = f32[1,1920,2048]{2,0,1:T(1,128)} async-done(((f32[1,1920,2048]{2,0,1:T(1,128)}), f32[1,1920,2048]{2,0,1:T(1,128)}, u32[]{:S(2)}, u32[]{:S(2)}) %all-to-all-start.1) | async-done | bytes 15728672 | tf_op jit(solution)/shard_map/all_to_all | solution.py:198
  1342.7 18.9 copy.241
  1361.6 18.2 gather_fusion.1
  1394.3 140.6 %all-reduce.11.cloned.1.call-done = (f32[192,2048]{1,0:T(8,128)}, f32[192,2048]{1,0:T(8,128)}) async-done(((f32[192,2048]{1,0:T(8,128)}, f32[192,2048]{1,0:T(8,128)}), (f32[192,2048]{1,0:T(8,128)}, f32[192,2048]{1,0:T(8,128)})) %all-reduce.11.cloned.1.call-update) | async-done | bytes 3145744 | tf_op jit(solution)/shard_map/psum | solution.py:212
  1568.6 22.1 %reduce-scatter.9.cloned.1.call-done = f32[192,1024]{1,0:T(8,128)} async-done(((f32[768,1024]{1,0:T(8,128)}), f32[192,1024]{1,0:T(8,128)}) %reduce-scatter.9.cloned.1.call-update) | async-done | bytes 786448 | tf_op jit(solution)/shard_map/reduce_scatter | solution.py:260
  1602.9 28.7 %reduce-scatter.11.cloned.1.call-done = f32[192,1024]{1,0:T(8,128)} async-done(((f32[768,1024]{1,0:T(8,128)}), f32[192,1024]{1,0:T(8,128)}) %reduce-scatter.11.cloned.1.call-update) | async-done | bytes 786448 | tf_op jit(solution)/shard_map/reduce_scatter | solution.py:263
  1648.5 29.4 %all-reduce.9.cloned.1.call-done = bf16[192,2048]{1,0:T(8,128)(2,1)} async-done(((bf16[192,2048]{1,0:T(8,128)(2,1)}), bf16[192,2048]{1,0:T(8,128)(2,1)}) %all-reduce.9.cloned.1.call-update) | async-done | bytes 786448 | tf_op jit(solution)/shard_map/psum | solution.py:288
  1690.1 10.4 convolution_bitcast_fusion.2
  1700.5 24.7 %copy.148 = f32[3,2048,1024]{2,1,0:T(8,128)} copy(f32[3,2048,1024]{1,2,0:T(8,128)} %convolution_bitcast_fusion.2) | data formatting | bytes 50331648 | tf_op jit(solution)/shard_map/td,tjh->jdh/transpose | solution.py:283
  1726.8 12.1 convolution_bitcast_fusion.3
  1738.9 16.5 copy.150
  1768.2 25.7 %reduce-scatter.17.cloned.1.call-done = f32[128,16]{0,1:T(8,128)} async-done(((f32[2048,16]{0,1:T(8,128)}), f32[128,16]{0,1:T(8,128)}) %reduce-scatter.17.cloned.1.call-update) | async-done | bytes 8208 | tf_op jit(solution)/shard_map/reduce_scatter | solution.py:303
  1793.9 107.1 %reduce-scatter.15.cloned.1.call-done = f32[128,1024]{1,0:T(8,128)} async-done(((f32[2048,1024]{1,0:T(8,128)}), f32[128,1024]{1,0:T(8,128)}) %reduce-scatter.15.cloned.1.call-update) | async-done | bytes 524304 | tf_op jit(solution)/shard_map/reduce_scatter | solution.py:301
  1900.9 247.9 %reduce-scatter.13.cloned.1.call-done = f32[384,1024]{1,0:T(8,128)} async-done(((f32[6144,1024]{1,0:T(8,128)}), f32[384,1024]{1,0:T(8,128)}) %reduce-scatter.13.cloned.1.call-update) | async-done | bytes 1572880 | tf_op jit(solution)/shard_map/reduce_scatter | solution.py:300
  (303 shorter events, 232.9 us)
Async XLA Ops:
  7.2 632.1 %copy-start = (bf16[1,2048,512]{2,1,0:T(8,128)(2,1)S(1)}, bf16[1,2048,512]{2,1,0:T(8,128)(2,1)}, u32[]{:S(2)}) copy-start(bf16[1,2048,512]{2,1,0:T(8,128)(2,1)} %param.17) | copy-start | bytes 6291460
  7.2 106.3 %copy-start.7 = (bf16[192,2048]{1,0:T(8,128)(2,1)S(1)}, bf16[192,2048]{1,0:T(8,128)(2,1)}, u32[]{:S(2)}) copy-start(bf16[192,2048]{1,0:T(8,128)(2,1)} %param.11) | copy-start | bytes 2359300
  7.2 106.3 %all-gather.6.cloned.1.call-start = ((), (), s32[]{:S(2)}) async-start(), calls=%async_computation.10 | async-start | bytes 13369344 | tf_op jit(solution)/shard_map/all_gather | solution.py:71
  7.9 132.7 %all-gather.12.cloned.1.call-start = ((), (), s32[]{:S(2)}) async-start(), calls=%async_computation.20 | async-start | bytes 1966080 | tf_op jit(solution)/shard_map/all_gather | solution.py:121
  35.5 99.5 %copy-start.35 = (f32[192,128]{1,0:T(8,128)}, f32[192,128]{1,0:T(8,128)S(1)}, u32[]{:S(2)}) copy-start(f32[192,128]{1,0:T(8,128)S(1)} %get-tuple-element.88) | copy-start | bytes 294916
  37.0 82.6 %copy-start.55 = (f32[192]{0:T(256)}, f32[192]{0:T(256)S(1)}, u32[]{:S(2)}) copy-start(f32[192]{0:T(256)S(1)} %add_rsqrt_fusion.3) | copy-start | bytes 2308
  37.0 82.6 %copy-start.39 = (f32[2048,1]{0,1:T(1,128)}, f32[2048,1]{0,1:T(1,128)S(1)}, u32[]{:S(2)}) copy-start(f32[2048,1]{0,1:T(1,128)S(1)} %get-tuple-element.94) | copy-start | bytes 24580
  37.0 400.2 %copy-start.43 = (f32[2048,1]{0,1:T(1,128)}, f32[2048,1]{0,1:T(1,128)S(1)}, u32[]{:S(2)}) copy-start(f32[2048,1]{0,1:T(1,128)S(1)} %get-tuple-element.91) | copy-start | bytes 24580
  121.8 39.8 %all-gather.8.cloned.1.call-start = ((), (), s32[]{:S(2)}) async-start(), calls=%async_computation.11 | async-start | bytes 1966080 | tf_op jit(solution)/shard_map/all_gather | solution.py:120
  139.6 74.4 %all-gather.10.cloned.1.call-start = ((), (), s32[]{:S(2)}) async-start(), calls=%async_computation.12 | async-start | bytes 4456448 | tf_op jit(solution)/shard_map/all_gather | solution.py:72
  140.2 129.0 %all-reduce.7.cloned.1.call-start = ((), (), s32[]{:S(2)}) async-start(), calls=%async_computation.13 | async-start | bytes 3145728 | tf_op jit(solution)/shard_map/psum | solution.py:145
  168.4 50.6 %copy-start.27 = (bf16[8,24,8,128]{3,2,1,0:T(8,128)(2,1)}, bf16[8,24,8,128]{3,2,1,0:T(8,128)(2,1)S(1)}, u32[]{:S(2)}) copy-start(bf16[8,24,8,128]{3,2,1,0:T(8,128)(2,1)S(1)} %fusion.57) | copy-start | bytes 1179652
  168.4 50.6 %copy-start.47 = (s32[192,8]{0,1:T(8,128)S(1)}, s32[192,8]{0,1:T(8,128)}, u32[]{:S(2)}) copy-start(s32[192,8]{0,1:T(8,128)} %param.18) | copy-start | bytes 18436
  270.9 166.3 %copy-start.57 = (f32[192]{0:T(256)}, f32[192]{0:T(256)S(1)}, u32[]{:S(2)}) copy-start(f32[192]{0:T(256)S(1)} %add_rsqrt_fusion) | copy-start | bytes 2308
  288.0 167.8 %all-to-all-start = ((bf16[16,120,2048]{2,1,0:T(8,128)(2,1)}), bf16[16,120,2048]{2,1,0:T(8,128)(2,1)}, u32[]{:S(2)}, u32[]{:S(2)}) async-start(bf16[16,120,2048]{2,1,0:T(8,128)(2,1)} %broadcast_select_fusion), calls=%async_computation | async-start | bytes 15728640 | tf_op jit(solution)/shard_map/all_to_all | solution.py:173
  455.7 183.6 %all-to-all-start.2 = ((bf16[16,120,2048]{2,1,0:T(8,128)(2,1)}), bf16[16,120,2048]{2,1,0:T(8,128)(2,1)}, u32[]{:S(2)}, u32[]{:S(2)}) async-start(bf16[16,120,2048]{2,1,0:T(8,128)(2,1)} %fusion), calls=%async_computation.2 | async-start | bytes 15728640 | tf_op jit(solution)/shard_map/all_to_all | solution.py:174
  684.6 313.6 %all-to-all-start.3 = ((f32[1,1920,2048]{2,0,1:T(1,128)}), f32[1,1920,2048]{2,0,1:T(1,128)}, u32[]{:S(2)}, u32[]{:S(2)}) async-start(f32[1,1920,2048]{2,0,1:T(1,128)} %copy.137), calls=%async_computation.3 | async-start | bytes 31457280 | tf_op jit(solution)/shard_map/all_to_all | solution.py:199
  998.3 344.4 %all-to-all-start.1 = ((f32[1,1920,2048]{2,0,1:T(1,128)}), f32[1,1920,2048]{2,0,1:T(1,128)}, u32[]{:S(2)}, u32[]{:S(2)}) async-start(f32[1,1920,2048]{2,0,1:T(1,128)} %copy.134), calls=%async_computation.1 | async-start | bytes 31457280 | tf_op jit(solution)/shard_map/all_to_all | solution.py:198
  1064.3 470.5 %all-reduce.11.cloned.1.call-start = ((), (), s32[]{:S(2)}) async-start(), calls=%async_computation.22 | async-start | bytes 6291456 | tf_op jit(solution)/shard_map/psum | solution.py:212
  1388.4 146.5 %copy-start.6 = (f32[192,2048]{1,0:T(8,128)S(1)}, f32[192,2048]{1,0:T(8,128)}, u32[]{:S(2)}) copy-start(f32[192,2048]{1,0:T(8,128)} %copy-done.5) | copy-start | bytes 4718596
  1388.4 146.5 %copy-start.38 = (bf16[2048,16]{0,1:T(8,128)(2,1)S(1)}, bf16[2048,16]{0,1:T(8,128)(2,1)}, u32[]{:S(2)}) copy-start(bf16[2048,16]{0,1:T(8,128)(2,1)} %copy-done.37) | copy-start | bytes 196612
  1388.4 146.5 %copy-start.44 = (f32[2048,1]{0,1:T(1,128)S(1)}, f32[2048,1]{0,1:T(1,128)}, u32[]{:S(2)}) copy-start(f32[2048,1]{0,1:T(1,128)} %copy-done.43) | copy-start | bytes 24580
  1388.4 146.4 %copy-start.58 = (f32[192]{0:T(256)S(1)}, f32[192]{0:T(256)}, u32[]{:S(2)}) copy-start(f32[192]{0:T(256)} %copy-done.57) | copy-start | bytes 2308
  1388.5 202.2 %reduce-scatter.9.cloned.1.call-start = ((), (), s32[]{:S(2)}) async-start(), calls=%async_computation.14 | async-start | bytes 3932160 | tf_op jit(solution)/shard_map/reduce_scatter | solution.py:260
  1552.6 79.0 %reduce-scatter.11.cloned.1.call-start = ((), (), s32[]{:S(2)}) async-start(), calls=%async_computation.15 | async-start | bytes 3932160 | tf_op jit(solution)/shard_map/reduce_scatter | solution.py:263
  1561.4 116.6 %all-reduce.9.cloned.1.call-start = ((), (), s32[]{:S(2)}) async-start(), calls=%async_computation.16 | async-start | bytes 1572864 | tf_op jit(solution)/shard_map/psum | solution.py:288
  1633.6 44.4 %copy-start.56 = (f32[192]{0:T(256)S(1)}, f32[192]{0:T(256)}, u32[]{:S(2)}) copy-start(f32[192]{0:T(256)} %copy-done.55) | copy-start | bytes 2308
  1643.4 123.3 %reduce-scatter.19.cloned.1.call-start = ((), (), s32[]{:S(2)}) async-start(), calls=%async_computation.21 | async-start | bytes 1114112
  1681.2 112.7 %reduce-scatter.17.cloned.1.call-start = ((), (), s32[]{:S(2)}) async-start(), calls=%async_computation.19 | async-start | bytes 139264 | tf_op jit(solution)/shard_map/reduce_scatter | solution.py:303
  1683.0 217.9 %reduce-scatter.15.cloned.1.call-start = ((), (), s32[]{:S(2)}) async-start(), calls=%async_computation.18 | async-start | bytes 8912896 | tf_op jit(solution)/shard_map/reduce_scatter | solution.py:301
  1689.1 459.8 %reduce-scatter.13.cloned.1.call-start = ((), (), s32[]{:S(2)}) async-start(), calls=%async_computation.17 | async-start | bytes 26738688 | tf_op jit(solution)/shard_map/reduce_scatter | solution.py:300
  1765.1 383.7 %copy-start.1 = (bf16[1,2048,512]{2,1,0:T(8,128)(2,1)S(1)}, bf16[1,2048,512]{2,1,0:T(8,128)(2,1)}, u32[]{:S(2)}) copy-start(bf16[1,2048,512]{2,1,0:T(8,128)(2,1)} %param.17) | copy-start | bytes 6291460
  (60 other events, 471.1 us)
Sparse Core Ops, SparseCore 0:
  10.3 103.1 all-gather.5
  121.9 17.8 all-gather.11
  142.0 19.6 all-gather.7
  163.7 50.3 all-gather.9
  219.1 50.0 all-reduce.6
  1388.6 146.2 all-reduce.10
  1552.7 37.8 reduce-scatter.8
  1593.7 37.8 reduce-scatter.10
  1643.5 34.3 all-reduce.8
  1681.4 57.5 reduce-scatter.18
  1743.0 50.8 reduce-scatter.16
  1798.4 102.5 reduce-scatter.14
  1905.6 243.1 reduce-scatter.12
where the time goes:
time: 2170 us; the launch traced here: 2160 us
  waiting for transfers between devices  1390 us (64%)
  local copies, waits for them, and re-layouts  224 us (10%)
  blocking collectives  179 us (8%)
  starting transfers between devices  150 us (7%)
  matrix products  126 us (6%)
  other arithmetic  74.3 us (3%)
    reduce_scatter x1, waiting for transfers between devices, local(): lax.psum_scatter(qkv_grad, ('shard', 'ctx'), scatter_dimension=0, tiled=T...  248 us
    all_to_all x1, waiting for transfers between devices, local(): lax.all_to_all(mid_part, ('shard', 'ctx'), split_axis=1, concat_axis=0, t...  247 us
    all_to_all x1, waiting for transfers between devices, local(): lax.all_to_all(expert_part, ('shard', 'ctx'), split_axis=1, concat_axis=0...  232 us
    psum x1, waiting for transfers between devices, local(): lax.psum((mixture_part, grad_part, score_part), 'tp')  141 us
    all_gather x1, blocking collectives, local(): lax.all_gather(router, ('shard', 'ctx'), axis=0, tiled=True)  135 us
    all_to_all x1, waiting for transfers between devices, local(): lax.all_to_all(send_grad, ('shard', 'ctx'), split_axis=0, concat_axis=1,...  128 us
    reduce_scatter x1, waiting for transfers between devices, local(): lax.psum_scatter(out_proj_grad, ('shard', 'ctx'), scatter_dimension=0, ti...  107 us
    unnamed x159, local copies, waits for them, and re-layouts  76.6 us
  transfers between devices with their start and end apart: 17, of which 14 were waited for; matrix products, arithmetic and copies ran while one was open for 12% of the time, Pallas kernels for 0%

commit v1 on v0

--- a/solution.py
+++ b/solution.py
@@ -7,6 +7,28 @@
 norm_eps = 1e-05
 rope_base = 10000.0
 masked_score = -1e30
+
+
+def in_blocks(x, dim, peers):
+    before, after = (x.shape[:dim], x.shape[dim + 1 :])
+    return jnp.moveaxis(x.reshape(*before, peers, -1, *after), dim, 0)
+
+
+def laid_out(pieces, dim):
+    lengths = list(pieces.shape[1:])
+    lengths[dim] *= pieces.shape[0]
+    return jnp.moveaxis(pieces, 0, dim).reshape(lengths)
+
+
+def swapped_with_each(shard, axis, split_dim, concat_dim):
+    devices, index = (lax.axis_size(axis), lax.axis_index(axis))
+    blocks = in_blocks(shard, split_dim, devices)
+    finished = [blocks[index]]
+    for lap in range(1, devices):
+        sent = blocks[index ^ lap]
+        finished.append(lax.ppermute(sent, axis, [(i, i ^ lap) for i in range(devices)]))
+    blocks = jnp.stack(finished)[index ^ jnp.arange(devices)]
+    return laid_out(blocks, concat_dim)
 
 
 def places_info(order_row, length_row):
@@ -196,7 +218,7 @@
     out_grad_f = out_grad.astype(jnp.float32)
     back_rows, back_grads = (
         lax.all_to_all(expert_part, ("shard", "ctx"), split_axis=1, concat_axis=0, tiled=True),
-        lax.all_to_all(mid_part, ("shard", "ctx"), split_axis=1, concat_axis=0, tiled=True),
+        swapped_with_each(mid_part, ("shard", "ctx"), 1, 0),
     )
     columns = back_rows.shape[-1]
     rows_y = back_rows.reshape(experts * capacity, columns)[slot_dest].reshape(

time: 2170 us -> 2180 us (level)
    ppermute x0 -> x15, waiting for transfers between devices: none -> 552 us  [swapped_with_each(): lax.ppermute(sent, axis, [(i, i ^ lap) for i in range(devices)])]
    all_to_all x1 -> x0, waiting for transfers between devices: 247 us -> none  [local(): lax.all_to_all(mid_part, ('shard', 'ctx'), split_axis=1, concat_axis=0, t...]
    all_to_all x1, waiting for transfers between devices: 232 us -> 0.01 us  [local(): lax.all_to_all(expert_part, ('shard', 'ctx'), split_axis=1, concat_axis=0...]
    ppermute x0 -> x15, starting transfers between devices: none -> 76.7 us  [swapped_with_each(): lax.ppermute(sent, axis, [(i, i ^ lap) for i in range(devices)])]
    psum x1, waiting for transfers between devices: 141 us -> 95 us  [local(): lax.psum((mixture_part, grad_part, score_part), 'tp')]
    all_to_all x1 -> x0, starting transfers between devices: 35.3 us -> none  [local(): lax.all_to_all(mid_part, ('shard', 'ctx'), split_axis=1, concat_axis=0, t...]
    all_to_all x1, starting transfers between devices: 66 us -> 35 us  [local(): lax.all_to_all(expert_part, ('shard', 'ctx'), split_axis=1, concat_axis=0...]
    all_to_all x1, waiting for transfers between devices: 128 us -> 97.9 us  [local(): lax.all_to_all(send_grad, ('shard', 'ctx'), split_axis=0, concat_axis=1,...]
  transfers between devices with their start and end apart: 17 -> 31, of which waited for: 14 -> 24; matrix products, arithmetic and copies ran while one was open for 12% -> 14% of each run, Pallas kernels for 0% -> 0%
where the time goes in v1:
time: 2180 us; the launch traced here: 2170 us
  waiting for transfers between devices  1390 us (64%)
  local copies, waits for them, and re-layouts  233 us (11%)
  blocking collectives  179 us (8%)
  starting transfers between devices  161 us (7%)
  matrix products  123 us (6%)
  other arithmetic  71.1 us (3%)
    ppermute x15, waiting for transfers between devices, swapped_with_each(): lax.ppermute(sent, axis, [(i, i ^ lap) for i in range(devices)])  552 us
    reduce_scatter x1, waiting for transfers between devices, local(): lax.psum_scatter(qkv_grad, ('shard', 'ctx'), scatter_dimension=0, tiled=T...  248 us
    all_gather x1, blocking collectives, local(): lax.all_gather(router, ('shard', 'ctx'), axis=0, tiled=True)  135 us
    reduce_scatter x1, waiting for transfers between devices, local(): lax.psum_scatter(out_proj_grad, ('shard', 'ctx'), scatter_dimension=0, ti...  107 us
    all_to_all x1, waiting for transfers between devices, local(): lax.all_to_all(send_grad, ('shard', 'ctx'), split_axis=0, concat_axis=1,...  97.9 us
    psum x1, waiting for transfers between devices, local(): lax.psum((mixture_part, grad_part, score_part), 'tp')  95 us
    unnamed x193, local copies, waits for them, and re-layouts  81.2 us
    ppermute x15, starting transfers between devices, swapped_with_each(): lax.ppermute(sent, axis, [(i, i ^ lap) for i in range(devices)])  76.7 us
  transfers between devices with their start and end apart: 31, of which 24 were waited for; matrix products, arithmetic and copies ran while one was open for 14% of the time, Pallas kernels for 0%

profile of v1, /device:TPU:0, one launch (start us, length us, event | category | flops | bytes accessed | tf_op | source)
XLA Modules:
  0.0 2168.5 jit_solution(3319242667779410353)
XLA Ops:
  10.3 23.8 %all_gather.18 = bf16[2048,4]{0,1:T(4,128)(2,1)S(1)} all-gather(bf16[128,4]{0,1:T(4,128)(2,1)} %param.14), channel_id=1, replica_groups=mesh['shard'=4,'ctx'=4,'tp'=2] {'shard','ctx'}, dimensions={0}, use_global_device_ids=true | all-gather | bytes 17408 | tf_op jit(solution)/shard_map/all_gather | solution.py:95
  37.0 76.5 %all-gather.6.cloned.1.call-done = bf16[6144,1024]{1,0:T(8,128)(2,1)} async-done(((bf16[384,1024]{1,0:T(8,128)(2,1)}), bf16[6144,1024]{1,0:T(8,128)(2,1)}) %all-gather.6.cloned.1.call-update) | async-done | bytes 12582928 | tf_op jit(solution)/shard_map/all_gather | solution.py:93
  143.1 18.8 all-gather.8.cloned.1.call-done
  168.6 45.6 %all-gather.10.cloned.1.call-done = bf16[2048,1024]{1,0:T(8,128)(2,1)} async-done(((bf16[128,1024]{1,0:T(8,128)(2,1)}), bf16[2048,1024]{1,0:T(8,128)(2,1)}) %all-gather.10.cloned.1.call-update) | async-done | bytes 4194320 | tf_op jit(solution)/shard_map/all_gather | solution.py:94
  231.6 37.8 %all-reduce.7.cloned.1.call-done = f32[192,2048]{1,0:T(8,128)} async-done(((f32[192,2048]{1,0:T(8,128)}), f32[192,2048]{1,0:T(8,128)}) %all-reduce.7.cloned.1.call-update) | async-done | bytes 1572880 | tf_op jit(solution)/shard_map/psum | solution.py:167
  302.7 134.7 %all_gather.23 = bf16[2048,16]{0,1:T(8,128)(2,1)S(1)} all-gather(bf16[128,16]{0,1:T(8,128)(2,1)S(1)} %copy-done.81), channel_id=1, replica_groups=mesh['shard'=4,'ctx'=4,'tp'=2] {'shard','ctx'}, dimensions={0}, use_global_device_ids=true | all-gather | bytes 69632 | tf_op jit(solution)/shard_map/all_gather | solution.py:96
  455.8 42.3 %all-to-all-start.2 = ((bf16[16,120,2048]{2,1,0:T(8,128)(2,1)}), bf16[16,120,2048]{2,1,0:T(8,128)(2,1)}, u32[]{:S(2)}, u32[]{:S(2)}) async-start(bf16[16,120,2048]{2,1,0:T(8,128)(2,1)} %fusion), calls=%async_computation.2 | async-start | bytes 15728640 | tf_op jit(solution)/shard_map/all_to_all | solution.py:196
  519.0 22.7 %copy.134 = f32[1,1920,2048]{2,0,1:T(1,128)} copy(f32[1,1920,2048]{2,1,0:T(8,128)S(1)} %convolution_bitcast_fusion) | data formatting | bytes 31457280 | tf_op jit(solution)/shard_map/erf,edf->erd/dot_general | solution.py:204
  541.7 97.9 %all-to-all-done.2 = bf16[16,120,2048]{2,1,0:T(8,128)(2,1)} async-done(((bf16[16,120,2048]{2,1,0:T(8,128)(2,1)}), bf16[16,120,2048]{2,1,0:T(8,128)(2,1)}, u32[]{:S(2)}, u32[]{:S(2)}) %all-to-all-start.2) | async-done | bytes 7864352 | tf_op jit(solution)/shard_map/all_to_all | solution.py:196
  639.6 35.0 %all-to-all-start.1 = ((f32[1,1920,2048]{2,0,1:T(1,128)}), f32[1,1920,2048]{2,0,1:T(1,128)}, u32[]{:S(2)}, u32[]{:S(2)}) async-start(f32[1,1920,2048]{2,0,1:T(1,128)} %copy.134), calls=%async_computation.1 | async-start | bytes 31457280 | tf_op jit(solution)/shard_map/all_to_all | solution.py:220
  725.4 59.4 %collective-permute-done.1 = f32[1,120,2048]{2,1,0:T(8,128)} collective-permute-done((f32[1,120,2048]{2,1,0:T(8,128)}, f32[1,120,2048]{2,1,0:T(8,128)}, u32[]{:S(2)}, u32[]{:S(2)}) %collective-permute-start.1) | collective-permute-done | bytes 983072 | tf_op jit(solution)/shard_map/ppermute | solution.py:29
  787.1 39.5 %collective-permute-done.2 = f32[1,120,2048]{2,1,0:T(8,128)S(1)} collective-permute-done((f32[1,120,2048]{2,1,0:T(8,128)}, f32[1,120,2048]{2,1,0:T(8,128)S(1)}, u32[]{:S(2)}, u32[]{:S(2)}) %collective-permute-start.2) | collective-permute-done | bytes 983072 | tf_op jit(solution)/shard_map/ppermute | solution.py:29
  827.7 185.4 %collective-permute-done.3 = f32[1,120,2048]{2,1,0:T(8,128)S(1)} collective-permute-done((f32[1,120,2048]{2,1,0:T(8,128)S(1)}, f32[1,120,2048]{2,1,0:T(8,128)S(1)}, u32[]{:S(2)}, u32[]{:S(2)}) %collective-permute-start.3) | collective-permute-done | bytes 983072 | tf_op jit(solution)/shard_map/ppermute | solution.py:29
  1019.0 15.2 collective-permute-done.4
  1039.8 19.1 collective-permute-done.5
  1058.9 23.8 %collective-permute-start.7 = (f32[1,120,2048]{2,1,0:T(8,128)S(1)}, f32[1,120,2048]{2,1,0:T(8,128)S(1)}, u32[]{:S(2)}, u32[]{:S(2)}) collective-permute-start(f32[1,120,2048]{2,1,0:T(8,128)S(1)} %copy-done.40), channel_id=1, source_target_pairs={{0,16},{2,18},{4,20},{6,22},{8,24},{10,26},{12,28},{14,30},{16,0},... | collective-permute-start | bytes 2949128 | tf_op jit(solution)/shard_map/ppermute | solution.py:29
  1104.4 113.1 %collective-permute-done.7 = f32[1,120,2048]{2,1,0:T(8,128)S(1)} collective-permute-done((f32[1,120,2048]{2,1,0:T(8,128)S(1)}, f32[1,120,2048]{2,1,0:T(8,128)S(1)}, u32[]{:S(2)}, u32[]{:S(2)}) %collective-permute-start.7) | collective-permute-done | bytes 983072 | tf_op jit(solution)/shard_map/ppermute | solution.py:29
  1227.0 31.4 %collective-permute-done.8 = f32[1,120,2048]{2,1,0:T(8,128)S(1)} collective-permute-done((f32[1,120,2048]{2,1,0:T(8,128)S(1)}, f32[1,120,2048]{2,1,0:T(8,128)S(1)}, u32[]{:S(2)}, u32[]{:S(2)}) %collective-permute-start.8) | collective-permute-done | bytes 983072 | tf_op jit(solution)/shard_map/ppermute | solution.py:29
  1267.8 64.0 %collective-permute-done.9 = f32[1,120,2048]{2,1,0:T(8,128)S(1)} collective-permute-done((f32[1,120,2048]{2,1,0:T(8,128)S(1)}, f32[1,120,2048]{2,1,0:T(8,128)S(1)}, u32[]{:S(2)}, u32[]{:S(2)}) %collective-permute-start.9) | collective-permute-done | bytes 983072 | tf_op jit(solution)/shard_map/ppermute | solution.py:29
  1335.2 16.4 collective-permute-done.10
  1373.7 18.2 gather_fusion.4
  1400.6 18.8 copy.240
  1419.4 18.3 gather_fusion.1
  1451.8 95.0 %all-reduce.11.cloned.1.call-done = (f32[192,2048]{1,0:T(8,128)}, f32[192,2048]{1,0:T(8,128)}) async-done(((f32[192,2048]{1,0:T(8,128)}, f32[192,2048]{1,0:T(8,128)}), (f32[192,2048]{1,0:T(8,128)}, f32[192,2048]{1,0:T(8,128)})) %all-reduce.11.cloned.1.call-update) | async-done | bytes 3145744 | tf_op jit(solution)/shard_map/psum | solution.py:234
  1582.4 21.1 reduce-scatter.9.cloned.1.call-done
  1616.1 28.4 %reduce-scatter.11.cloned.1.call-done = f32[192,1024]{1,0:T(8,128)} async-done(((f32[768,1024]{1,0:T(8,128)}), f32[192,1024]{1,0:T(8,128)}) %reduce-scatter.11.cloned.1.call-update) | async-done | bytes 786448 | tf_op jit(solution)/shard_map/reduce_scatter | solution.py:285
  1661.4 29.4 %all-reduce.9.cloned.1.call-done = bf16[192,2048]{1,0:T(8,128)(2,1)} async-done(((bf16[192,2048]{1,0:T(8,128)(2,1)}), bf16[192,2048]{1,0:T(8,128)(2,1)}) %all-reduce.9.cloned.1.call-update) | async-done | bytes 786448 | tf_op jit(solution)/shard_map/psum | solution.py:310
  1713.4 24.8 %copy.147 = f32[3,2048,1024]{2,1,0:T(8,128)} copy(f32[3,2048,1024]{1,2,0:T(8,128)} %convolution_bitcast_fusion.1) | data formatting | bytes 50331648 | tf_op jit(solution)/shard_map/td,tjh->jdh/transpose | solution.py:305
  1752.0 16.5 copy.149
  1781.2 25.6 %reduce-scatter.17.cloned.1.call-done = f32[128,16]{0,1:T(8,128)} async-done(((f32[2048,16]{0,1:T(8,128)}), f32[128,16]{0,1:T(8,128)}) %reduce-scatter.17.cloned.1.call-update) | async-done | bytes 8208 | tf_op jit(solution)/shard_map/reduce_scatter | solution.py:325
  1806.8 107.0 %reduce-scatter.15.cloned.1.call-done = f32[128,1024]{1,0:T(8,128)} async-done(((f32[2048,1024]{1,0:T(8,128)}), f32[128,1024]{1,0:T(8,128)}) %reduce-scatter.15.cloned.1.call-update) | async-done | bytes 524304 | tf_op jit(solution)/shard_map/reduce_scatter | solution.py:323
  1913.8 247.9 %reduce-scatter.13.cloned.1.call-done = f32[384,1024]{1,0:T(8,128)} async-done(((f32[6144,1024]{1,0:T(8,128)}), f32[384,1024]{1,0:T(8,128)}) %reduce-scatter.13.cloned.1.call-update) | async-done | bytes 1572880 | tf_op jit(solution)/shard_map/reduce_scatter | solution.py:322
  (370 shorter events, 399.3 us)
Async XLA Ops:
  7.2 507.5 %copy-start = (bf16[1,2048,512]{2,1,0:T(8,128)(2,1)S(1)}, bf16[1,2048,512]{2,1,0:T(8,128)(2,1)}, u32[]{:S(2)}) copy-start(bf16[1,2048,512]{2,1,0:T(8,128)(2,1)} %param.17) | copy-start | bytes 6291460
  7.2 106.3 %all-gather.6.cloned.1.call-start = ((), (), s32[]{:S(2)}) async-start(), calls=%async_computation.9 | async-start | bytes 13369344 | tf_op jit(solution)/shard_map/all_gather | solution.py:93
  7.9 132.1 %all-gather.12.cloned.1.call-start = ((), (), s32[]{:S(2)}) async-start(), calls=%async_computation.19 | async-start | bytes 1966080 | tf_op jit(solution)/shard_map/all_gather | solution.py:143
  122.0 39.8 %all-gather.8.cloned.1.call-start = ((), (), s32[]{:S(2)}) async-start(), calls=%async_computation.10 | async-start | bytes 1966080 | tf_op jit(solution)/shard_map/all_gather | solution.py:142
  137.3 77.0 %all-gather.10.cloned.1.call-start = ((), (), s32[]{:S(2)}) async-start(), calls=%async_computation.11 | async-start | bytes 4456448 | tf_op jit(solution)/shard_map/all_gather | solution.py:94
  137.9 131.5 %all-reduce.7.cloned.1.call-start = ((), (), s32[]{:S(2)}) async-start(), calls=%async_computation.12 | async-start | bytes 3145728 | tf_op jit(solution)/shard_map/psum | solution.py:167
  288.2 167.6 %all-to-all-start = ((bf16[16,120,2048]{2,1,0:T(8,128)(2,1)}), bf16[16,120,2048]{2,1,0:T(8,128)(2,1)}, u32[]{:S(2)}, u32[]{:S(2)}) async-start(bf16[16,120,2048]{2,1,0:T(8,128)(2,1)} %broadcast_select_fusion), calls=%async_computation | async-start | bytes 15728640 | tf_op jit(solution)/shard_map/all_to_all | solution.py:195
  455.8 183.8 %all-to-all-start.2 = ((bf16[16,120,2048]{2,1,0:T(8,128)(2,1)}), bf16[16,120,2048]{2,1,0:T(8,128)(2,1)}, u32[]{:S(2)}, u32[]{:S(2)}) async-start(bf16[16,120,2048]{2,1,0:T(8,128)(2,1)} %fusion), calls=%async_computation.2 | async-start | bytes 15728640 | tf_op jit(solution)/shard_map/all_to_all | solution.py:196
  639.6 761.0 %all-to-all-start.1 = ((f32[1,1920,2048]{2,0,1:T(1,128)}), f32[1,1920,2048]{2,0,1:T(1,128)}, u32[]{:S(2)}, u32[]{:S(2)}) async-start(f32[1,1920,2048]{2,0,1:T(1,128)} %copy.134), calls=%async_computation.1 | async-start | bytes 31457280 | tf_op jit(solution)/shard_map/all_to_all | solution.py:220
  674.6 872.1 %all-reduce.11.cloned.1.call-start = ((), (), s32[]{:S(2)}) async-start(), calls=%async_computation.21 | async-start | bytes 6291456 | tf_op jit(solution)/shard_map/psum | solution.py:234
  710.6 12.0 collective-permute-start
  711.0 73.8 %collective-permute-start.1 = (f32[1,120,2048]{2,1,0:T(8,128)}, f32[1,120,2048]{2,1,0:T(8,128)}, u32[]{:S(2)}, u32[]{:S(2)}) collective-permute-start(f32[1,120,2048]{2,1,0:T(8,128)} %get-tuple-element.83), channel_id=1, source_target_pairs={{0,4},{2,6},{4,0},{6,2},{8,12},{10,14},{12,8},{14,10},{16,20},{18,... | collective-permute-start | bytes 2949128 | tf_op jit(solution)/shard_map/ppermute | solution.py:29
  712.9 646.6 %collective-permute-start.14 = (f32[1,120,2048]{2,1,0:T(8,128)}, f32[1,120,2048]{2,1,0:T(8,128)S(1)}, u32[]{:S(2)}, u32[]{:S(2)}) collective-permute-start(f32[1,120,2048]{2,1,0:T(8,128)} %get-tuple-element.70), channel_id=1, source_target_pairs={{0,30},{2,28},{4,26},{6,24},{8,22},{10,20},{12,18},{14,16},{16,14}... | collective-permute-start | bytes 2949128 | tf_op jit(solution)/shard_map/ppermute | solution.py:29
  715.9 642.5 %collective-permute-start.13 = (f32[1,120,2048]{2,1,0:T(8,128)}, f32[1,120,2048]{2,1,0:T(8,128)S(1)}, u32[]{:S(2)}, u32[]{:S(2)}) collective-permute-start(f32[1,120,2048]{2,1,0:T(8,128)} %get-tuple-element.71), channel_id=1, source_target_pairs={{0,28},{2,30},{4,24},{6,26},{8,20},{10,22},{12,16},{14,18},{16,12}... | collective-permute-start | bytes 2949128 | tf_op jit(solution)/shard_map/ppermute | solution.py:29
  717.4 640.0 %collective-permute-start.12 = (f32[1,120,2048]{2,1,0:T(8,128)}, f32[1,120,2048]{2,1,0:T(8,128)S(1)}, u32[]{:S(2)}, u32[]{:S(2)}) collective-permute-start(f32[1,120,2048]{2,1,0:T(8,128)} %get-tuple-element.72), channel_id=1, source_target_pairs={{0,26},{2,24},{4,30},{6,28},{8,18},{10,16},{12,22},{14,20},{16,10}... | collective-permute-start | bytes 2949128 | tf_op jit(solution)/shard_map/ppermute | solution.py:29
  722.6 104.0 %collective-permute-start.2 = (f32[1,120,2048]{2,1,0:T(8,128)}, f32[1,120,2048]{2,1,0:T(8,128)S(1)}, u32[]{:S(2)}, u32[]{:S(2)}) collective-permute-start(f32[1,120,2048]{2,1,0:T(8,128)} %get-tuple-element.82), channel_id=1, source_target_pairs={{0,6},{2,4},{4,2},{6,0},{8,14},{10,12},{12,10},{14,8},{16,22},{18,... | collective-permute-start | bytes 2949128 | tf_op jit(solution)/shard_map/ppermute | solution.py:29
  784.8 228.3 %collective-permute-start.3 = (f32[1,120,2048]{2,1,0:T(8,128)S(1)}, f32[1,120,2048]{2,1,0:T(8,128)S(1)}, u32[]{:S(2)}, u32[]{:S(2)}) collective-permute-start(f32[1,120,2048]{2,1,0:T(8,128)S(1)} %copy-done.43), channel_id=1, source_target_pairs={{0,8},{2,10},{4,12},{6,14},{8,0},{10,2},{12,4},{14,6},{16,24},{18,... | collective-permute-start | bytes 2949128 | tf_op jit(solution)/shard_map/ppermute | solution.py:29
  826.6 207.7 %collective-permute-start.4 = (f32[1,120,2048]{2,1,0:T(8,128)}, f32[1,120,2048]{2,1,0:T(8,128)S(1)}, u32[]{:S(2)}, u32[]{:S(2)}) collective-permute-start(f32[1,120,2048]{2,1,0:T(8,128)} %get-tuple-element.80), channel_id=1, source_target_pairs={{0,10},{2,8},{4,14},{6,12},{8,2},{10,0},{12,6},{14,4},{16,26},{18,... | collective-permute-start | bytes 2949128 | tf_op jit(solution)/shard_map/ppermute | solution.py:29
  1013.1 45.8 %collective-permute-start.5 = (f32[1,120,2048]{2,1,0:T(8,128)S(1)}, f32[1,120,2048]{2,1,0:T(8,128)S(1)}, u32[]{:S(2)}, u32[]{:S(2)}) collective-permute-start(f32[1,120,2048]{2,1,0:T(8,128)S(1)} %copy-done.42), channel_id=1, source_target_pairs={{0,12},{2,14},{4,8},{6,10},{8,4},{10,6},{12,0},{14,2},{16,28},{18,... | collective-permute-start | bytes 2949128 | tf_op jit(solution)/shard_map/ppermute | solution.py:29
  1034.3 54.8 %collective-permute-start.6 = (f32[1,120,2048]{2,1,0:T(8,128)S(1)}, f32[1,120,2048]{2,1,0:T(8,128)S(1)}, u32[]{:S(2)}, u32[]{:S(2)}) collective-permute-start(f32[1,120,2048]{2,1,0:T(8,128)S(1)} %copy-done.41), channel_id=1, source_target_pairs={{0,14},{2,12},{4,10},{6,8},{8,6},{10,4},{12,2},{14,0},{16,30},{18,... | collective-permute-start | bytes 2949128 | tf_op jit(solution)/shard_map/ppermute | solution.py:29
  1058.9 158.6 %collective-permute-start.7 = (f32[1,120,2048]{2,1,0:T(8,128)S(1)}, f32[1,120,2048]{2,1,0:T(8,128)S(1)}, u32[]{:S(2)}, u32[]{:S(2)}) collective-permute-start(f32[1,120,2048]{2,1,0:T(8,128)S(1)} %copy-done.40), channel_id=1, source_target_pairs={{0,16},{2,18},{4,20},{6,22},{8,24},{10,26},{12,28},{14,30},{16,0},... | collective-permute-start | bytes 2949128 | tf_op jit(solution)/shard_map/ppermute | solution.py:29
  1089.0 169.4 %collective-permute-start.8 = (f32[1,120,2048]{2,1,0:T(8,128)S(1)}, f32[1,120,2048]{2,1,0:T(8,128)S(1)}, u32[]{:S(2)}, u32[]{:S(2)}) collective-permute-start(f32[1,120,2048]{2,1,0:T(8,128)S(1)} %copy-done.39), channel_id=1, source_target_pairs={{0,18},{2,16},{4,22},{6,20},{8,26},{10,24},{12,30},{14,28},{16,2},... | collective-permute-start | bytes 2949128 | tf_op jit(solution)/shard_map/ppermute | solution.py:29
  1217.5 114.3 %collective-permute-start.9 = (f32[1,120,2048]{2,1,0:T(8,128)S(1)}, f32[1,120,2048]{2,1,0:T(8,128)S(1)}, u32[]{:S(2)}, u32[]{:S(2)}) collective-permute-start(f32[1,120,2048]{2,1,0:T(8,128)S(1)} %copy-done.38), channel_id=1, source_target_pairs={{0,20},{2,22},{4,16},{6,18},{8,28},{10,30},{12,24},{14,26},{16,4},... | collective-permute-start | bytes 2949128 | tf_op jit(solution)/shard_map/ppermute | solution.py:29
  1258.4 93.2 %collective-permute-start.10 = (f32[1,120,2048]{2,1,0:T(8,128)S(1)}, f32[1,120,2048]{2,1,0:T(8,128)S(1)}, u32[]{:S(2)}, u32[]{:S(2)}) collective-permute-start(f32[1,120,2048]{2,1,0:T(8,128)S(1)} %copy-done.37), channel_id=1, source_target_pairs={{0,22},{2,20},{4,18},{6,16},{8,30},{10,28},{12,26},{14,24},{16,6},... | collective-permute-start | bytes 2949128 | tf_op jit(solution)/shard_map/ppermute | solution.py:29
  1331.8 24.5 %collective-permute-start.11 = (f32[1,120,2048]{2,1,0:T(8,128)S(1)}, f32[1,120,2048]{2,1,0:T(8,128)S(1)}, u32[]{:S(2)}, u32[]{:S(2)}) collective-permute-start(f32[1,120,2048]{2,1,0:T(8,128)S(1)} %copy-done.36), channel_id=1, source_target_pairs={{0,24},{2,26},{4,28},{6,30},{8,16},{10,18},{12,20},{14,22},{16,8},... | collective-permute-start | bytes 2949128 | tf_op jit(solution)/shard_map/ppermute | solution.py:29
  1446.4 157.1 %reduce-scatter.9.cloned.1.call-start = ((), (), s32[]{:S(2)}) async-start(), calls=%async_computation.13 | async-start | bytes 3932160 | tf_op jit(solution)/shard_map/reduce_scatter | solution.py:282
  1565.4 79.1 %reduce-scatter.11.cloned.1.call-start = ((), (), s32[]{:S(2)}) async-start(), calls=%async_computation.14 | async-start | bytes 3932160 | tf_op jit(solution)/shard_map/reduce_scatter | solution.py:285
  1574.2 116.5 %all-reduce.9.cloned.1.call-start = ((), (), s32[]{:S(2)}) async-start(), calls=%async_computation.15 | async-start | bytes 1572864 | tf_op jit(solution)/shard_map/psum | solution.py:310
  1656.3 123.4 %reduce-scatter.19.cloned.1.call-start = ((), (), s32[]{:S(2)}) async-start(), calls=%async_computation.20 | async-start | bytes 1114112
  1694.0 112.8 %reduce-scatter.17.cloned.1.call-start = ((), (), s32[]{:S(2)}) async-start(), calls=%async_computation.18 | async-start | bytes 139264 | tf_op jit(solution)/shard_map/reduce_scatter | solution.py:325
  1695.9 218.0 %reduce-scatter.15.cloned.1.call-start = ((), (), s32[]{:S(2)}) async-start(), calls=%async_computation.17 | async-start | bytes 8912896 | tf_op jit(solution)/shard_map/reduce_scatter | solution.py:323
  1701.9 459.8 %reduce-scatter.13.cloned.1.call-start = ((), (), s32[]{:S(2)}) async-start(), calls=%async_computation.16 | async-start | bytes 26738688 | tf_op jit(solution)/shard_map/reduce_scatter | solution.py:322
  (84 other events, 4382.5 us)
Sparse Core Ops, SparseCore 0:
  10.3 103.1 all-gather.5
  122.1 17.8 all-gather.11
  142.2 19.6 all-gather.7
  163.9 50.3 all-gather.9
  219.3 50.0 all-reduce.6
  1446.5 100.1 all-reduce.10
  1565.5 37.8 reduce-scatter.8
  1606.6 37.8 reduce-scatter.10
  1656.4 34.3 all-reduce.8
  1694.3 57.5 reduce-scatter.18
  1755.8 50.9 reduce-scatter.16
  1811.3 102.4 reduce-scatter.14
  1918.5 243.1 reduce-scatter.12
